TPU v7x, 128 devices: a whole 4x4x4 slice. The times are simulated.
128 devices in a mesh: slab: 16 (over x_hi, z, core), col: 8 (over x_lo, y).
Axes of the slice: x: 4 (x_hi: 2, x_lo: 2; x = x_hi * 2 + x_lo), y: 4, z: 4, core: 2. Of those that a mesh axis runs over, the one named last changes fastest.
Arguments:
- sensitivity: bfloat16 [3, 512, 65536], P(None, 'col', 'slab'), may hold values from -0.03125 to 0.03125
- residual_force: bfloat16 [3, 65536], P(None, 'slab'), may hold values from -6 to 6
- moments: float32 [6, 64, 1024], P(None, 'slab'), as said below
- zone_label: int32 [64, 1024], P('slab'), may hold values from 0 to 511, as said below
- misfit: float32 [64, 1024], P('slab'), may hold values from 0.1 to 10
Outputs:
- hessian: float32 [512, 512], P('col', 'slab')
- gradient: float32 [512], replicated
- zone_misfit: float32 [512], replicated
Inputs may be any that keep to these rules, and one draw needn't show every extreme that they name: zone_label is the box of a 8 x 8 x 8 partition of the specimen that holds the element, the in-plane box borders displaced by at most one element; every zone occurs. `moments`: each element's moment matrix is symmetric with positive diagonal, and each diagonal entry exceeds the sum of the magnitudes of the others in its row.
All inputs are finite; a program needn't handle non-finite values.
Results may differ from a plain program's by a relative error of at most 0.0003.
Values may be sent and summed in bfloat16 or wider, within the bound.
A program may use at most 128 MiB of HBM per device.

v0:
```python
import jax
import jax.numpy as jnp
from jax import lax
from jax.sharding import PartitionSpec as P

GX = 64
GY = 16
third = 1.0 / 3.0
sixth = 1.0 / 6.0


def shifted(value, axis, by):
    count = lax.axis_size(axis)
    pairs = [(i, i + by) for i in range(count) if 0 <= i + by < count]
    return lax.ppermute(value, axis, pairs)


def mix_pair(first, second):
    return (third * first + sixth * second, sixth * first + third * second)


def shift_ahead(field, step, keep):
    moved = jnp.concatenate([field[..., step:], jnp.zeros_like(field[..., :step])], axis=-1)
    if keep is None:
        return moved
    return jnp.where(keep, moved, 0.0)


def shift_behind(field, step, keep):
    moved = jnp.concatenate([jnp.zeros_like(field[..., :step]), field[..., :-step]], axis=-1)
    if keep is None:
        return moved
    return jnp.where(keep, moved, 0.0)


def apply_moments(moments, field):
    comps = [moments[k][None, :] for k in range(6)]
    first, second, last = (field[0], field[1], field[2])
    out_x = comps[0] * first + comps[3] * second + comps[4] * last
    out_y = comps[3] * first + comps[1] * second + comps[5] * last
    out_z = comps[4] * first + comps[5] * second + comps[2] * last
    return jnp.stack([out_x, out_y, out_z])


def element_layer(lower, upper, moments):
    plane = lower.shape[-1]
    pos_y = jnp.arange(plane, dtype=jnp.int32) % GY
    not_last = pos_y != GY - 1
    not_first = pos_y != 0
    mixed_z = mix_pair(lower, upper)
    results = []
    for side_z in range(2):
        field = mixed_z[side_z]
        mixed_x = mix_pair(field, shift_ahead(field, GY, None))
        values = []
        for side_x in range(2):
            layer = mixed_x[side_x]
            mixed_y = mix_pair(layer, shift_ahead(layer, 1, not_last))
            values.append([apply_moments(moments, mixed_y[side_y]) for side_y in range(2)])
        total = values[0][0]
        total = total + shift_behind(values[1][0], GY, None)
        total = total + shift_behind(values[0][1], 1, not_first)
        total = total + shift_behind(shift_behind(values[1][1], 1, not_first), GY, None)
        results.append(total)
    return (results[0], results[1])


def on_device(sensitivity, residual_force, moments, zone_label, misfit):
    cols = sensitivity.shape[1]
    layers = moments.shape[1]
    plane_size = GX * GY
    n_slab = lax.axis_size("slab")
    n_col = lax.axis_size("col")
    width = cols * n_col
    field = sensitivity.reshape(3, cols, layers, plane_size)
    above = shifted(sensitivity[:, :, :plane_size], "slab", -1)
    levels = []
    carry = None
    first_lower = None
    for level in range(layers):
        lower = field[:, :, level].astype(jnp.float32)
        if level + 1 < layers:
            upper = field[:, :, level + 1].astype(jnp.float32)
        else:
            upper = above.astype(jnp.float32)
        to_lower, to_upper = element_layer(lower, upper, moments[:, level])
        if level == 0:
            first_lower = to_lower
        else:
            levels.append((carry + to_lower).astype(jnp.bfloat16))
        carry = to_upper
    from_below = shifted(carry.astype(jnp.bfloat16), "slab", 1).astype(carry.dtype)
    levels.insert(0, (from_below + first_lower).astype(jnp.bfloat16))
    image = jnp.stack(levels, axis=2).reshape(3, cols, layers * plane_size)
    panel_rows = lax.dot_general(
        image,
        lax.all_gather(sensitivity, "col", axis=1, tiled=True),
        (((0, 2), (0, 2)), ((), ())),
        preferred_element_type=jnp.float32,
    )
    hessian = lax.psum_scatter(panel_rows, "slab", scatter_dimension=1, tiled=True)
    grad_part = lax.dot_general(
        residual_force,
        sensitivity,
        (((0, 1), (0, 2)), ((), ())),
        preferred_element_type=jnp.float32,
    )
    grad_full = lax.dynamic_update_slice_in_dim(
        jnp.zeros((width,), jnp.float32), grad_part, lax.axis_index("col") * cols, 0
    )
    elements = layers * plane_size
    share = elements // n_col
    offset = lax.axis_index("col") * share
    zone_part = lax.dynamic_slice_in_dim(zone_label.reshape(elements), offset, share, 0)
    misfit_part = lax.dynamic_slice_in_dim(misfit.reshape(elements), offset, share, 0)
    onehot = (zone_part[:, None] == jnp.arange(width, dtype=jnp.int32)[None, :]).astype(jnp.float32)
    zone_part_sum = jnp.dot(misfit_part, onehot, precision=lax.Precision.HIGHEST)
    gradient, zone_sums = lax.psum((grad_full, zone_part_sum), ("slab", "col"))
    zone_misfit = zone_sums * (width / (elements * n_slab))
    return (hessian, gradient, zone_misfit)


def solution(mesh):
    in_specs = (
        P(None, "col", "slab"),
        P(None, "slab"),
        P(None, "slab", None),
        P("slab", None),
        P("slab", None),
    )
    out_specs = (P("col", "slab"), P(), P())
    return jax.shard_map(
        on_device, mesh=mesh, in_specs=in_specs, out_specs=out_specs, check_vma=False
    )
```

profile of v0, /device:TPU:0, one launch (start us, length us, event | category | flops | bytes accessed | tf_op | source)
XLA Modules:
  0.0 330.2 jit_solution(12702796365399645540)
XLA Ops:
  7.2 0.7 all-gather.2.cloned.1.call-update
  8.0 0.6 copy-done
  8.6 0.8 slice.768
  9.3 1.3 collective-permute-start
  10.6 1.2 reshape.1815
  11.8 3.2 fusion.94
  15.0 0.9 copy-done.1
  15.9 0.4 fusion.8
  16.3 0.9 copy-done.3
  17.2 1.2 slice.966
  18.5 0.5 convolution_bitcast_fusion.1
  19.1 0.5 fusion
  19.5 1.4 fusion.96
  21.0 1.2 fusion.14
  22.2 1.3 multiply_add_fusion.41
  23.4 0.6 fusion.92
  24.0 1.4 slice.1015
  25.4 2.3 slice.999
  27.7 1.2 slice.967
  28.9 1.2 slice.971
  30.2 161.3 %all-reduce.56 = (f32[512]{0:T(512)}, f32[512]{0:T(512)}) all-reduce(f32[512]{0:T(512)S(1)} %dynamic_update_slice.3, f32[512]{0:T(512)S(1)} %bitcast.370), channel_id=1, replica_groups=mesh['slab'=16,'col'=8] {'slab','col'}, use_global_device_ids=true, to_apply=%region_1.2 | all-reduce | flops 1024 | bytes 8192 | tf_op jit(solution)/shard_map/psum | solution.py:118
  191.6 0.6 fusion.91
  192.2 0.7 fusion.95
  192.8 1.5 fusion.3
  194.6 1.2 fusion.5
  196.2 2.6 multiply_add_fusion.45
  199.0 0.3 slice.1047
  199.3 0.6 multiply_add_fusion.17
  199.9 1.2 slice.1048
  201.1 1.2 slice.1052
  202.3 1.2 slice.1064
  203.4 1.1 slice.1068
  204.6 1.2 slice.953
  206.1 0.3 multiply_add_fusion.35
  206.4 1.1 slice.983
  207.6 1.2 slice.987
  208.7 1.2 slice.1000
  209.9 1.2 slice.949
  211.1 1.2 slice.1004
  212.2 1.2 slice.1016
  213.4 1.2 slice.1020
  214.6 1.1 slice.1032
  215.7 1.2 slice.1036
  216.9 5.2 %multiply_add_fusion.42 = (f32[3,64,1024]{2,1,0:T(8,128)}, f32[3,64,1024]{2,1,0:T(8,128)}, f32[3,64,1024]{2,1,0:T(8,128)S(1)}, f32[3,64,1024]{2,1,0:T(8,128)S(1)...) fusion(f32[3,64,1024]{2,1,0:T(8,128)S(1)} %get-tuple-element.43, ...), kind=kLoop, calls=%fused_computation.212 | loop fusion | flops 8257536 | bytes 18870784 | tf_op jit(solution)/shard_map/add | solution.py:19
  222.1 2.1 multiply_add_fusion.122
  224.2 0.9 multiply_add_fusion.110
  225.2 5.7 %multiply_add_fusion.46 = (f32[3,64,1024]{2,1,0:T(8,128)}, f32[3,64,1024]{2,1,0:T(8,128)}, f32[3,64,1024]{2,1,0:T(8,128)}, f32[3,64,1024]{2,1,0:T(8,128)S(1)}, f...) fusion(f32[3,64,1024]{2,1,0:T(8,128)S(1)} %get-tuple-element.44, ...), kind=kLoop, calls=%fused_computation.217 | loop fusion | flops 8257536 | bytes 18870784 | tf_op jit(solution)/shard_map/add | solution.py:19
  231.0 1.3 multiply_add_fusion.98
  232.7 0.8 copy-done.10
  234.0 0.7 copy-done.9
  235.2 0.6 copy-done.20
  236.0 1.5 fusion.76
  237.6 0.7 fusion.81
  238.3 1.8 collective-permute-start.1
  240.2 1.0 multiply_add_fusion.10
  242.4 0.8 copy-done.5
  245.4 0.5 fusion.28
  245.9 1.4 fusion.87
  247.3 1.3 fusion.86
  248.6 1.3 fusion.85
  249.9 0.7 fusion.84
  251.0 7.1 %convolution_bitcast_fusion = f32[64,512]{0,1:T(8,128)} fusion(bf16[3,64,4096]{2,1,0:T(8,128)(2,1)S(1)} %bitcast.171, bf16[3,512,4096]{2,1,0:T(8,128)(2,1)} %all-gather.2.cloned.1.call-done), kind=kOutput, calls=%fused_computation.1 | convolution fusion | flops 805306368 | bytes 14286848 | tf_op jit(solution)/shard_map/dot_general | solution.py:95
  258.1 0.6 broadcast_multiply_fusion
  258.7 64.7 %reduce-scatter.2.cloned.1.call-done = f32[64,32]{0,1:T(8,128)} async-done(((f32[64,512]{0,1:T(8,128)}), f32[64,32]{0,1:T(8,128)}) %reduce-scatter.2.cloned.1.call-update) | async-done | bytes 8208 | tf_op jit(solution)/shard_map/reduce_scatter | solution.py:101
  (144 shorter events, 6.6 us)
Async XLA Ops:
  7.2 1.4 copy-start
  7.2 243.8 %all-gather.2.cloned.1.call-start = ((), (), s32[]{:S(2)}) async-start(), calls=%async_computation.1 | async-start | bytes 14155776 | tf_op jit(solution)/shard_map/all_gather | solution.py:97
  7.9 315.5 %reduce-scatter.2.cloned.1.call-start = ((), (), s32[]{:S(2)}) async-start(), calls=%async_computation.2 | async-start | bytes 278528 | tf_op jit(solution)/shard_map/reduce_scatter | solution.py:101
  9.3 183.5 %collective-permute-start = (bf16[3,64,1024]{2,1,0:T(8,128)(2,1)}, bf16[3,64,1024]{2,1,0:T(8,128)(2,1)}, u32[]{:S(2)}, u32[]{:S(2)}) collective-permute-start(bf16[3,64,1024]{2,1,0:T(8,128)(2,1)} %slice.768), channel_id=1, source_target_pairs={{8,0},{16,8},{24,16},{32,24},{40,32},{48,40},{56,48},{64,56},{72,6... | collective-permute-start | bytes 1179656 | tf_op jit(solution)/shard_map/ppermute | solution.py:15
  15.0 0.9 copy-start.1
  15.9 2.4 copy-start.47
  15.9 2.4 copy-start.48
  15.9 2.6 copy-start.51
  16.3 0.9 copy-start.3
  17.2 3.8 %copy-start.19 = (bf16[3,64,1,1024]{3,2,1,0:T(2,128)(2,1)S(1)}, bf16[3,64,1,1024]{3,2,1,0:T(2,128)(2,1)}, u32[]{:S(2)}) copy-start(bf16[3,64,1,1024]{3,2,1,0:T(2,128)(2,1)} %get-tuple-element.57) | copy-start | bytes 1179652
  19.1 3.1 copy-start.4
  19.1 3.1 copy-start.18
  27.7 164.5 %copy-start.45 = (f32[6,4,1024]{2,1,0:T(4,128)S(1)}, f32[6,4,1024]{2,1,0:T(4,128)}, u32[]{:S(2)}) copy-start(f32[6,4,1024]{2,1,0:T(4,128)} %param.7) | copy-start | bytes 294916
  194.6 1.5 copy-start.2
  194.6 1.5 copy-start.17
  214.6 2.3 copy-start.49
  216.9 5.2 %copy-start.25 = (f32[1,1,1024]{2,1,0:T(1,128)S(1)}, f32[1,1,1024]{2,1,0:T(1,128)}, u32[]{:S(2)}) copy-start(f32[1,1,1024]{2,1,0:T(1,128)} %get-tuple-element.188) | copy-start | bytes 12292
  216.9 5.2 %copy-start.26 = (f32[1,1,1024]{2,1,0:T(1,128)S(1)}, f32[1,1,1024]{2,1,0:T(1,128)}, u32[]{:S(2)}) copy-start(f32[1,1,1024]{2,1,0:T(1,128)} %get-tuple-element.189) | copy-start | bytes 12292
  222.1 2.1 copy-start.11
  225.2 5.7 %copy-start.29 = (f32[1,1,1024]{2,1,0:T(1,128)S(1)}, f32[1,1,1024]{2,1,0:T(1,128)}, u32[]{:S(2)}) copy-start(f32[1,1,1024]{2,1,0:T(1,128)} %get-tuple-element.179) | copy-start | bytes 12292
  225.2 5.7 %copy-start.30 = (f32[1,1,1024]{2,1,0:T(1,128)S(1)}, f32[1,1,1024]{2,1,0:T(1,128)}, u32[]{:S(2)}) copy-start(f32[1,1,1024]{2,1,0:T(1,128)} %get-tuple-element.180) | copy-start | bytes 12292
  225.2 5.7 %copy-start.31 = (f32[1,1,1024]{2,1,0:T(1,128)S(1)}, f32[1,1,1024]{2,1,0:T(1,128)}, u32[]{:S(2)}) copy-start(f32[1,1,1024]{2,1,0:T(1,128)} %get-tuple-element.181) | copy-start | bytes 12292
  225.2 5.7 %copy-start.32 = (f32[1,1,1024]{2,1,0:T(1,128)S(1)}, f32[1,1,1024]{2,1,0:T(1,128)}, u32[]{:S(2)}) copy-start(f32[1,1,1024]{2,1,0:T(1,128)} %get-tuple-element.182) | copy-start | bytes 12292
  225.2 5.7 %copy-start.33 = (f32[1,1,1024]{2,1,0:T(1,128)S(1)}, f32[1,1,1024]{2,1,0:T(1,128)}, u32[]{:S(2)}) copy-start(f32[1,1,1024]{2,1,0:T(1,128)} %get-tuple-element.183) | copy-start | bytes 12292
  225.2 5.7 %copy-start.34 = (f32[1,1,1024]{2,1,0:T(1,128)S(1)}, f32[1,1,1024]{2,1,0:T(1,128)}, u32[]{:S(2)}) copy-start(f32[1,1,1024]{2,1,0:T(1,128)} %get-tuple-element.184) | copy-start | bytes 12292
  230.9 1.5 copy-start.12
  230.9 1.6 copy-start.7
  230.9 1.6 copy-start.35
  231.0 1.6 copy-start.36
  231.0 1.6 copy-start.37
  231.0 1.6 copy-start.42
  231.0 1.6 copy-start.43
  231.0 1.6 copy-start.44
  232.4 1.2 copy-start.10
  232.6 1.2 copy-start.6
  233.5 1.2 copy-start.9
  233.8 1.2 copy-start.8
  233.8 1.2 copy-start.27
  233.8 1.2 copy-start.28
  233.8 1.2 copy-start.38
  233.8 1.2 copy-start.39
  233.8 1.2 copy-start.40
  233.8 1.2 copy-start.41
  234.7 1.0 copy-start.20
  234.7 1.1 copy-start.21
  234.7 1.2 copy-start.22
  234.7 1.2 copy-start.23
  234.7 1.3 copy-start.24
  234.7 1.3 copy-start.46
  237.6 2.6 copy-start.13
  237.6 2.6 copy-start.14
  237.6 2.6 copy-start.15
  237.6 2.6 copy-start.16
  238.3 11.5 %collective-permute-start.1 = (bf16[3,64,1024]{2,1,0:T(8,128)(2,1)S(1)}, bf16[3,64,1024]{2,1,0:T(8,128)(2,1)S(1)}, u32[]{:S(2)}, u32[]{:S(2)}) collective-permute-start(bf16[3,64,1024]{2,1,0:T(8,128)(2,1)S(1)} %fusion.81), channel_id=1, source_target_pairs={{0,8},{8,16},{16,24},{24,32},{32,40},{40,48},{48,56},{56,64},{64,7... | collective-permute-start | bytes 1179656 | tf_op jit(solution)/shard_map/ppermute | solution.py:15
  242.1 1.1 copy-start.5
  251.0 7.1 %copy-start.50 = (f32[512]{0:T(512)S(1)}, f32[512]{0:T(512)}, u32[]{:S(2)}) copy-start(f32[512]{0:T(512)} %get-tuple-element.4) | copy-start | bytes 6148
Sparse Core Ops, SparseCore 0:
  9.6 134.1 all-gather.1
  258.2 65.1 reduce-scatter.1
where the time goes:
time: 331 us; the launch traced here: 330 us
  blocking collectives  161 us (49%)
  waiting for transfers between devices  65.4 us (20%)
  other arithmetic  38.8 us (12%)
  local copies, waits for them, and re-layouts  38.6 us (12%)
  between operations  14.8 us (4%)
  matrix products  8.09 us (2%)
    psum x1, blocking collectives, on_device(): gradient, zone_sums = lax.psum((grad_full, zone_part_sum), ('slab', 'col'))  161 us
    reduce_scatter x1, waiting for transfers between devices, on_device(): lax.psum_scatter(panel_rows, 'slab', scatter_dimension=1, tiled=True)  64.7 us
    slice x24, local copies, waits for them, and re-layouts, shift_ahead(): field[..., step:]  24.9 us
    add x11, other arithmetic, mix_pair(): return (third * first + sixth * second, sixth * first + third * second)  21 us
    add x32, other arithmetic, apply_moments(): out_x = comps[0] * first + comps[3] * second + comps[4] * last  8.5 us
    dot_general x1, matrix products, on_device(): lax.dot_general(image, lax.all_gather(sensitivity, 'col', axis=1, tiled=T...  7.08 us
  transfers between devices with their start and end apart: 4, of which 1 were waited for; matrix products, arithmetic and copies ran while one was open for 22% of the time, Pallas kernels for 0%

commit v1 on v0

--- a/solution.py
+++ b/solution.py
@@ -115,7 +115,7 @@
     misfit_part = lax.dynamic_slice_in_dim(misfit.reshape(elements), offset, share, 0)
     onehot = (zone_part[:, None] == jnp.arange(width, dtype=jnp.int32)[None, :]).astype(jnp.float32)
     zone_part_sum = jnp.dot(misfit_part, onehot, precision=lax.Precision.HIGHEST)
-    gradient, zone_sums = lax.psum((grad_full, zone_part_sum), ("slab", "col"))
+    gradient, zone_sums = lax.psum(lax.psum((grad_full, zone_part_sum), "col"), axis_name="slab")
     zone_misfit = zone_sums * (width / (elements * n_slab))
     return (hessian, gradient, zone_misfit)
 

time: 331 us -> 230 us (0.69)
  blocking collectives: 161 us -> 61.9 us
    psum x1 -> x2, blocking collectives: 161 us -> 61.9 us  [the longest x1 41.2 us: on_device(): lax.psum(lax.psum((grad_full, zone_part_sum), 'col'), axis_name='slab')]
  transfers between devices with their start and end apart: 4 -> 4, of which waited for: 1 -> 1; matrix products, arithmetic and copies ran while one was open for 22% -> 32% of each run, Pallas kernels for 0% -> 0%
where the time goes in v1:
time: 230 us; the launch traced here: 229 us
  waiting for transfers between devices  64.2 us (28%)
  blocking collectives  61.9 us (27%)
  other arithmetic  38.8 us (17%)
  local copies, waits for them, and re-layouts  38.7 us (17%)
  between operations  14.8 us (6%)
  matrix products  8.1 us (4%)
  starting transfers between devices  2.8 us (1%)
    reduce_scatter x1, waiting for transfers between devices, on_device(): lax.psum_scatter(panel_rows, 'slab', scatter_dimension=1, tiled=True)  63.4 us
    psum x1, blocking collectives, on_device(): lax.psum(lax.psum((grad_full, zone_part_sum), 'col'), axis_name='slab')  41.2 us
    slice x24, local copies, waits for them, and re-layouts, shift_ahead(): field[..., step:]  25 us
    add x11, other arithmetic, mix_pair(): return (third * first + sixth * second, sixth * first + third * second)  21 us
    psum x1, blocking collectives, on_device(): lax.psum((grad_full, zone_part_sum), 'col')  20.7 us
    add x32, other arithmetic, apply_moments(): out_x = comps[0] * first + comps[3] * second + comps[4] * last  8.51 us
    dot_general x1, matrix products, on_device(): lax.dot_general(image, lax.all_gather(sensitivity, 'col', axis=1, tiled=T...  7.09 us
    unnamed x106, local copies, waits for them, and re-layouts  6.02 us
  transfers between devices with their start and end apart: 4, of which 1 were waited for; matrix products, arithmetic and copies ran while one was open for 32% of the time, Pallas kernels for 0%

profile of v1, /device:TPU:0, one launch (start us, length us, event | category | flops | bytes accessed | tf_op | source)
XLA Modules:
  0.0 229.3 jit_solution(16675689700365335274)
XLA Ops:
  7.2 0.7 all-gather.2.cloned.1.call-update
  8.0 0.6 copy-done
  8.6 0.8 slice.768
  9.3 1.3 collective-permute-start
  10.6 1.2 reshape.1815
  11.8 3.2 %fusion.94 = (bf16[3,64,1,1024]{3,2,1,0:T(2,128)(2,1)}, bf16[3,64,1,1024]{3,2,1,0:T(2,128)(2,1)S(1)}, bf16[3,64,1,1024]{3,2,1,0:T(2,128)(2,1)}, bf16[3,64,1,1024]{3,2,1,0:T(2,128)(2,1)S(1)}) fusion(bf16[3,64,4,1024]{3,2,1,0:T(4,128)(2,1)S(1)} %reshape.1815), kind=kLoop, calls=%fused_computation.332 | loop fusion | bytes 3145728 | tf_op jit(solution)/shard_map/slice | solution.py:83
  15.0 0.9 copy-done.1
  16.0 0.4 fusion.8
  16.3 0.9 copy-done.3
  17.2 1.2 slice.966
  18.6 0.5 convolution_bitcast_fusion.1
  19.1 0.5 fusion
  19.6 1.4 fusion.96
  21.0 1.2 fusion.14
  22.2 1.3 multiply_add_fusion.41
  23.5 0.6 fusion.92
  24.1 1.4 slice.1015
  25.5 2.3 %slice.999 = f32[3,64,1008]{2,1,0:T(8,128)} slice(f32[3,64,1024]{2,1,0:T(8,128)} %get-tuple-element.11), slice={[0:3], [0:64], [16:1024]} | slice | bytes 1548288 | tf_op jit(solution)/shard_map/slice | solution.py:23
  27.8 1.2 slice.967
  28.9 1.2 slice.971
  30.3 20.7 %all-reduce.57 = (f32[512]{0:T(512)S(1)}, f32[512]{0:T(512)S(1)}) all-reduce(f32[512]{0:T(512)S(1)} %dynamic_update_slice.3, f32[512]{0:T(512)S(1)} %bitcast.370), channel_id=1, replica_groups=mesh['slab'=16,'col'=8] {'col'}, use_global_device_ids=true, to_apply=%region_1.2 | all-reduce | flops 1024 | bytes 8192 | tf_op jit(solution)/shard_map/psum | solution.py:118
  51.0 41.2 %all-reduce.56 = (f32[512]{0:T(512)}, f32[512]{0:T(512)}) all-reduce(f32[512]{0:T(512)S(1)} %get-tuple-element.5, f32[512]{0:T(512)S(1)} %get-tuple-element.6), channel_id=1, replica_groups=mesh['slab'=16,'col'=8] {'slab'}, use_global_device_ids=true, to_apply=%region_2.3 | all-reduce | flops 1024 | bytes 8192 | tf_op jit(solution)/shard_map/psum | solution.py:118
  92.2 0.6 fusion.91
  92.8 0.7 fusion.95
  93.5 1.5 fusion.3
  95.3 1.3 fusion.5
  96.8 2.6 %multiply_add_fusion.45 = (f32[3,64,1024]{2,1,0:T(8,128)S(1)}, f32[3,64,1024]{2,1,0:T(8,128)S(1)}, f32[3,64,1024]{2,1,0:T(8,128)S(1)}, f32[3,64,1024]{2,1,0:T(8,...) fusion(f32[3,64,1008]{2,1,0:T(8,128)S(1)} %slice.948, ...), kind=kLoop, calls=%fused_computation.216 | loop fusion | flops 8847360 | bytes 13713408 | tf_op jit(solution)/shard_map/add | solution.py:19
  99.9 0.6 multiply_add_fusion.17
  100.6 1.2 slice.1048
  101.7 1.2 slice.1052
  102.9 1.2 slice.1064
  104.1 1.2 slice.1068
  105.3 1.2 slice.953
  106.8 0.3 multiply_add_fusion.35
  107.1 1.1 slice.983
  108.2 1.2 slice.987
  109.4 1.2 slice.1000
  110.6 1.1 slice.949
  111.7 1.2 slice.1004
  112.9 1.2 slice.1016
  114.1 1.2 slice.1020
  115.3 1.2 slice.1032
  116.4 1.2 slice.1036
  117.6 5.2 %multiply_add_fusion.42 = (f32[3,64,1024]{2,1,0:T(8,128)}, f32[3,64,1024]{2,1,0:T(8,128)}, f32[3,64,1024]{2,1,0:T(8,128)S(1)}, f32[3,64,1024]{2,1,0:T(8,128)S(1)...) fusion(f32[3,64,1024]{2,1,0:T(8,128)S(1)} %get-tuple-element.45, ...), kind=kLoop, calls=%fused_computation.212 | loop fusion | flops 8257536 | bytes 18870784 | tf_op jit(solution)/shard_map/add | solution.py:19
  122.8 2.2 multiply_add_fusion.122
  125.0 0.9 multiply_add_fusion.110
  125.9 5.7 %multiply_add_fusion.46 = (f32[3,64,1024]{2,1,0:T(8,128)}, f32[3,64,1024]{2,1,0:T(8,128)}, f32[3,64,1024]{2,1,0:T(8,128)}, f32[3,64,1024]{2,1,0:T(8,128)S(1)}, f...) fusion(f32[3,64,1024]{2,1,0:T(8,128)S(1)} %get-tuple-element.46, ...), kind=kLoop, calls=%fused_computation.217 | loop fusion | flops 8257536 | bytes 18870784 | tf_op jit(solution)/shard_map/add | solution.py:19
  131.7 1.3 multiply_add_fusion.98
  133.5 0.8 copy-done.10
  134.7 0.7 copy-done.9
  135.9 0.6 copy-done.20
  136.8 1.5 fusion.76
  138.3 0.7 fusion.81
  139.0 1.4 collective-permute-start.1
  140.5 1.0 multiply_add_fusion.10
  142.7 0.8 copy-done.5
  145.8 0.5 fusion.28
  146.2 1.4 fusion.87
  147.6 1.3 fusion.86
  148.9 1.3 fusion.85
  150.2 0.7 fusion.84
  151.3 7.1 %convolution_bitcast_fusion = f32[64,512]{0,1:T(8,128)} fusion(bf16[3,64,4096]{2,1,0:T(8,128)(2,1)S(1)} %bitcast.171, bf16[3,512,4096]{2,1,0:T(8,128)(2,1)} %all-gather.2.cloned.1.call-done), kind=kOutput, calls=%fused_computation.1 | convolution fusion | flops 805306368 | bytes 14286848 | tf_op jit(solution)/shard_map/dot_general | solution.py:95
  158.4 0.6 broadcast_multiply_fusion
  159.0 63.4 %reduce-scatter.2.cloned.1.call-done = f32[64,32]{0,1:T(8,128)} async-done(((f32[64,512]{0,1:T(8,128)}), f32[64,32]{0,1:T(8,128)}) %reduce-scatter.2.cloned.1.call-update) | async-done | bytes 8208 | tf_op jit(solution)/shard_map/reduce_scatter | solution.py:101
  (145 shorter events, 6.9 us)
Async XLA Ops:
  7.2 1.4 copy-start
  7.2 144.1 %all-gather.2.cloned.1.call-start = ((), (), s32[]{:S(2)}) async-start(), calls=%async_computation.1 | async-start | bytes 14155776 | tf_op jit(solution)/shard_map/all_gather | solution.py:97
  7.9 214.5 %reduce-scatter.2.cloned.1.call-start = ((), (), s32[]{:S(2)}) async-start(), calls=%async_computation.2 | async-start | bytes 278528 | tf_op jit(solution)/shard_map/reduce_scatter | solution.py:101
  9.3 84.1 %collective-permute-start = (bf16[3,64,1024]{2,1,0:T(8,128)(2,1)}, bf16[3,64,1024]{2,1,0:T(8,128)(2,1)}, u32[]{:S(2)}, u32[]{:S(2)}) collective-permute-start(bf16[3,64,1024]{2,1,0:T(8,128)(2,1)} %slice.768), channel_id=1, source_target_pairs={{8,0},{16,8},{24,16},{32,24},{40,32},{48,40},{56,48},{64,56},{72,6... | collective-permute-start | bytes 1179656 | tf_op jit(solution)/shard_map/ppermute | solution.py:15
  15.0 0.9 copy-start.1
  15.9 2.5 %copy-start.47 = (f32[4,1024]{1,0:T(4,128)S(1)}, f32[4,1024]{1,0:T(4,128)}, u32[]{:S(2)}) copy-start(f32[4,1024]{1,0:T(4,128)} %param.9) | copy-start | bytes 49156
  15.9 2.5 %copy-start.48 = (s32[4,1024]{1,0:T(4,128)S(1)}, s32[4,1024]{1,0:T(4,128)}, u32[]{:S(2)}) copy-start(s32[4,1024]{1,0:T(4,128)} %param.8) | copy-start | bytes 49156
  16.0 2.6 %copy-start.51 = (bf16[3,4096]{1,0:T(4,128)(2,1)S(1)}, bf16[3,4096]{1,0:T(4,128)(2,1)}, u32[]{:S(2)}) copy-start(bf16[3,4096]{1,0:T(4,128)(2,1)} %param.6) | copy-start | bytes 73732
  16.3 0.9 copy-start.3
  17.2 3.8 %copy-start.19 = (bf16[3,64,1,1024]{3,2,1,0:T(2,128)(2,1)S(1)}, bf16[3,64,1,1024]{3,2,1,0:T(2,128)(2,1)}, u32[]{:S(2)}) copy-start(bf16[3,64,1,1024]{3,2,1,0:T(2,128)(2,1)} %get-tuple-element.59) | copy-start | bytes 1179652
  19.1 3.1 %copy-start.4 = (f32[3,64,1024]{2,1,0:T(8,128)S(1)}, f32[3,64,1024]{2,1,0:T(8,128)}, u32[]{:S(2)}) copy-start(f32[3,64,1024]{2,1,0:T(8,128)} %copy-done.3) | copy-start | bytes 2359300
  19.1 3.1 %copy-start.18 = (f32[3,64,1008]{2,1,0:T(8,128)S(1)}, f32[3,64,1008]{2,1,0:T(8,128)}, u32[]{:S(2)}) copy-start(f32[3,64,1008]{2,1,0:T(8,128)} %slice.966) | copy-start | bytes 2322436
  27.8 65.0 %copy-start.45 = (f32[6,4,1024]{2,1,0:T(4,128)S(1)}, f32[6,4,1024]{2,1,0:T(4,128)}, u32[]{:S(2)}) copy-start(f32[6,4,1024]{2,1,0:T(4,128)} %param.7) | copy-start | bytes 294916
  95.3 1.5 copy-start.2
  95.3 1.5 copy-start.17
  115.3 2.3 %copy-start.49 = (pred[1024]{0:T(1024)(128)(4,1)S(1)}, pred[1024]{0:T(1024)(128)(4,1)}, u32[]{:S(2)}) copy-start(pred[1024]{0:T(1024)(128)(4,1)} %fusion.92) | copy-start | bytes 3076
  117.6 5.2 %copy-start.25 = (f32[1,1,1024]{2,1,0:T(1,128)S(1)}, f32[1,1,1024]{2,1,0:T(1,128)}, u32[]{:S(2)}) copy-start(f32[1,1,1024]{2,1,0:T(1,128)} %get-tuple-element.190) | copy-start | bytes 12292
  117.6 5.2 %copy-start.26 = (f32[1,1,1024]{2,1,0:T(1,128)S(1)}, f32[1,1,1024]{2,1,0:T(1,128)}, u32[]{:S(2)}) copy-start(f32[1,1,1024]{2,1,0:T(1,128)} %get-tuple-element.191) | copy-start | bytes 12292
  122.8 2.2 copy-start.11
  125.9 5.7 %copy-start.29 = (f32[1,1,1024]{2,1,0:T(1,128)S(1)}, f32[1,1,1024]{2,1,0:T(1,128)}, u32[]{:S(2)}) copy-start(f32[1,1,1024]{2,1,0:T(1,128)} %get-tuple-element.181) | copy-start | bytes 12292
  125.9 5.7 %copy-start.30 = (f32[1,1,1024]{2,1,0:T(1,128)S(1)}, f32[1,1,1024]{2,1,0:T(1,128)}, u32[]{:S(2)}) copy-start(f32[1,1,1024]{2,1,0:T(1,128)} %get-tuple-element.182) | copy-start | bytes 12292
  125.9 5.7 %copy-start.31 = (f32[1,1,1024]{2,1,0:T(1,128)S(1)}, f32[1,1,1024]{2,1,0:T(1,128)}, u32[]{:S(2)}) copy-start(f32[1,1,1024]{2,1,0:T(1,128)} %get-tuple-element.183) | copy-start | bytes 12292
  125.9 5.7 %copy-start.32 = (f32[1,1,1024]{2,1,0:T(1,128)S(1)}, f32[1,1,1024]{2,1,0:T(1,128)}, u32[]{:S(2)}) copy-start(f32[1,1,1024]{2,1,0:T(1,128)} %get-tuple-element.184) | copy-start | bytes 12292
  125.9 5.7 %copy-start.33 = (f32[1,1,1024]{2,1,0:T(1,128)S(1)}, f32[1,1,1024]{2,1,0:T(1,128)}, u32[]{:S(2)}) copy-start(f32[1,1,1024]{2,1,0:T(1,128)} %get-tuple-element.185) | copy-start | bytes 12292
  125.9 5.7 %copy-start.34 = (f32[1,1,1024]{2,1,0:T(1,128)S(1)}, f32[1,1,1024]{2,1,0:T(1,128)}, u32[]{:S(2)}) copy-start(f32[1,1,1024]{2,1,0:T(1,128)} %get-tuple-element.186) | copy-start | bytes 12292
  131.6 1.5 copy-start.12
  131.7 1.6 copy-start.7
  131.7 1.6 copy-start.35
  131.7 1.6 copy-start.36
  131.7 1.6 copy-start.37
  131.7 1.6 copy-start.42
  131.7 1.6 copy-start.43
  131.7 1.6 copy-start.44
  133.1 1.2 copy-start.10
  133.3 1.2 copy-start.6
  134.2 1.2 copy-start.9
  134.5 1.2 copy-start.8
  134.5 1.2 copy-start.27
  134.5 1.2 copy-start.28
  134.5 1.2 copy-start.38
  134.5 1.2 copy-start.39
  134.5 1.2 copy-start.40
  134.5 1.2 copy-start.41
  135.4 1.0 copy-start.20
  135.4 1.1 copy-start.21
  135.4 1.2 copy-start.22
  135.4 1.2 copy-start.23
  135.4 1.3 copy-start.24
  135.5 1.3 copy-start.46
  138.3 2.2 copy-start.13
  138.3 2.2 copy-start.14
  138.3 2.2 copy-start.15
  138.3 2.2 copy-start.16
  139.0 11.1 %collective-permute-start.1 = (bf16[3,64,1024]{2,1,0:T(8,128)(2,1)S(1)}, bf16[3,64,1024]{2,1,0:T(8,128)(2,1)S(1)}, u32[]{:S(2)}, u32[]{:S(2)}) collective-permute-start(bf16[3,64,1024]{2,1,0:T(8,128)(2,1)S(1)} %fusion.81), channel_id=1, source_target_pairs={{0,8},{8,16},{16,24},{24,32},{32,40},{40,48},{48,56},{56,64},{64,7... | collective-permute-start | bytes 1179656 | tf_op jit(solution)/shard_map/ppermute | solution.py:15
  142.4 1.1 copy-start.5
  151.3 7.1 %copy-start.50 = (f32[512]{0:T(512)S(1)}, f32[512]{0:T(512)}, u32[]{:S(2)}) copy-start(f32[512]{0:T(512)} %get-tuple-element.4) | copy-start | bytes 6148
Sparse Core Ops, SparseCore 0:
  9.6 134.3 all-gather.1
  158.5 63.8 reduce-scatter.1
